TPU v7x, 512 devices: a whole 4x4x16 slice. The times are simulated.
512 devices in a mesh: expert: 128 (over y, x_lo, z), half: 4 (over x_hi, core).
Axes of the slice: x: 4 (x_hi: 2, x_lo: 2; x = x_hi * 2 + x_lo), y: 4, z: 16, core: 2. Of those that a mesh axis runs over, the one named last changes fastest.
Arguments:
- tokens: bfloat16 [25088, 1024], P('expert', 'half'), may hold values from -128 to 128
- slot_params: bfloat16 [1024, 256], P('half'), may hold values from -0.5 to 0.5
- w_up: bfloat16 [128, 1024, 4096], P('expert', None, 'half'), may hold values from -0.1875 to 0.1875
- w_down: bfloat16 [128, 4096, 1024], P('expert', 'half'), may hold values from -0.09375 to 0.09375
- cotangent: bfloat16 [25088, 1024], P('expert', 'half'), may hold values from -6 to 6
Outputs:
- mixed: bfloat16 [25088, 1024], P('expert', 'half')
- grad_tokens: bfloat16 [25088, 1024], P('expert', 'half')
- grad_params: float32 [1024, 256], P('half')
All inputs are finite; a program needn't handle non-finite values.
Results may differ from a plain program's by a relative error of at most 0.017.
Values may be sent and summed in bfloat16 or wider, within the bound.
A program may use at most 64 MiB of HBM per device.

v0:
```python
import jax
import jax.numpy as jnp
from jax import lax
from jax.sharding import PartitionSpec as P

SEQ = 196
SLOTS = 2
EXPERT = ("y", "x_lo", "z")
HALF = ("x_hi", "core")


def gelu_grad(preact, upstream):
    pullback = jax.vjp(jax.nn.gelu, preact)[1]
    return pullback(upstream)[0]


def softmax_back(probabilities, upstream, over_axis):
    inner = jnp.sum(probabilities * upstream, axis=over_axis, keepdims=True)
    return probabilities * (upstream - inner)


def local(tokens, slot_params, w_up, w_down, cotangent):
    feat_quarter = tokens.shape[1]
    images = tokens.shape[0] // SEQ
    columns = slot_params.shape[1]
    experts = columns // SLOTS
    up_matrix = w_up[0]
    down_matrix = w_down[0]
    inputs = tokens.reshape(images, SEQ, feat_quarter)
    upstream = cotangent.reshape(images, SEQ, feat_quarter)
    partial_logits = jnp.einsum(
        "imf,fc->imc", inputs, slot_params, preferred_element_type=jnp.float32
    )
    logits = lax.psum(partial_logits, HALF)
    dispatch = jax.nn.softmax(logits, axis=1)
    combine = jax.nn.softmax(logits, axis=2)
    dispatch_bf = dispatch.astype(jnp.bfloat16).reshape(images, SEQ, experts, SLOTS)
    combine_bf = combine.astype(jnp.bfloat16).reshape(images, SEQ, experts, SLOTS)
    slot_in = jnp.einsum(
        "imes,imf->sife", dispatch_bf, inputs, preferred_element_type=jnp.float32
    ).astype(jnp.bfloat16)
    received = lax.all_to_all(slot_in, EXPERT, split_axis=3, concat_axis=3, tiled=True)
    up_slice = up_matrix
    preact = jnp.einsum(
        "sifr,fk->sirk",
        lax.all_gather(received, HALF, axis=2, tiled=True),
        up_slice,
        preferred_element_type=jnp.float32,
    )
    hidden = jax.nn.gelu(preact).astype(jnp.bfloat16)
    down_slice = down_matrix
    summed = lax.psum(
        jnp.einsum("kf,sirk->fsir", down_slice, hidden, preferred_element_type=jnp.float32).astype(
            jnp.bfloat16
        ),
        HALF,
    ).astype(jnp.float32)
    slot_out = lax.dynamic_slice_in_dim(
        summed, lax.axis_index(HALF) * feat_quarter, feat_quarter, 0
    )
    returned = lax.all_to_all(
        slot_out.astype(jnp.bfloat16), EXPERT, split_axis=3, concat_axis=3, tiled=True
    )
    mixed = jnp.einsum(
        "imes,fsie->imf", combine_bf, returned, preferred_element_type=jnp.float32
    ).astype(jnp.bfloat16)
    grad_slot_out = jnp.einsum(
        "imes,imf->sife", combine_bf, upstream, preferred_element_type=jnp.float32
    ).astype(jnp.bfloat16)
    combine_part = jnp.einsum(
        "imf,fsie->imes", upstream, returned, preferred_element_type=jnp.float32
    ).reshape(images, SEQ, columns)
    grad_combine = lax.psum(combine_part.astype(jnp.bfloat16), HALF).astype(jnp.float32)
    grad_received = lax.all_to_all(grad_slot_out, EXPERT, split_axis=3, concat_axis=3, tiled=True)
    down_slice = down_matrix
    grad_hidden = jnp.einsum(
        "sifr,kf->sirk",
        lax.all_gather(grad_received, HALF, axis=2, tiled=True),
        down_slice,
        preferred_element_type=jnp.float32,
    )
    grad_preact = gelu_grad(preact, grad_hidden).astype(jnp.bfloat16)
    up_slice = up_matrix
    summed_grad = lax.psum(
        jnp.einsum(
            "fk,sirk->fsir", up_slice, grad_preact, preferred_element_type=jnp.float32
        ).astype(jnp.bfloat16),
        HALF,
    ).astype(jnp.float32)
    grad_slot_in = lax.dynamic_slice_in_dim(
        summed_grad, lax.axis_index(HALF) * feat_quarter, feat_quarter, 0
    )
    grad_returned = lax.all_to_all(
        grad_slot_in.astype(jnp.bfloat16), EXPERT, split_axis=3, concat_axis=3, tiled=True
    )
    dispatch_part = jnp.einsum(
        "imf,fsie->imes", inputs, grad_returned, preferred_element_type=jnp.float32
    ).reshape(images, SEQ, columns)
    grad_dispatch = lax.psum(dispatch_part.astype(jnp.bfloat16), HALF).astype(jnp.float32)
    grad_logits = softmax_back(combine, grad_combine, 2) + softmax_back(dispatch, grad_dispatch, 1)
    grad_logit_bf = grad_logits.astype(jnp.bfloat16)
    token_term = jnp.einsum(
        "imes,fsie->imf", dispatch_bf, grad_returned, preferred_element_type=jnp.float32
    )
    logit_term = jnp.einsum(
        "imc,fc->imf", grad_logit_bf, slot_params, preferred_element_type=jnp.float32
    )
    grad_tokens = (token_term + logit_term).astype(jnp.bfloat16).reshape(images * SEQ, feat_quarter)
    params_part = jnp.einsum(
        "imf,imc->fc", inputs, grad_logit_bf, preferred_element_type=jnp.float32
    )
    grad_params = lax.psum(lax.psum(lax.psum(params_part, "z"), "y"), "x_lo")
    return (mixed.reshape(images * SEQ, feat_quarter), grad_tokens, grad_params)


def solution(mesh):
    mesh = jax.sharding.Mesh(mesh.devices.reshape(4, 2, 16, 2, 2), EXPERT + HALF)
    in_specs = (
        P(EXPERT, HALF),
        P(HALF, None),
        P(EXPERT, None, HALF),
        P(EXPERT, HALF, None),
        P(EXPERT, HALF),
    )
    out_specs = (P(EXPERT, HALF), P(EXPERT, HALF), P(HALF, None))
    return jax.shard_map(local, mesh=mesh, in_specs=in_specs, out_specs=out_specs, check_vma=False)
```

profile of v0, /device:TPU:1, one launch (start us, length us, event | category | flops | bytes accessed | tf_op | source)
XLA Modules:
  0.0 566.3 jit_solution(11431547479652277655)
XLA Ops:
  7.2 2.0 convolution_bitcast_fusion.3
  9.2 64.2 %all-reduce.9.cloned.1.call-done = f32[1,196,256]{2,1,0:T(8,128)} async-done(((f32[1,196,256]{2,1,0:T(8,128)}), f32[1,196,256]{2,1,0:T(8,128)}) %all-reduce.9.cloned.1.call-update) | async-done | bytes 200720 | tf_op jit(solution)/shard_map/psum | solution.py:34
  73.4 1.0 fusion.82
  74.5 1.1 fusion.60
  75.6 1.1 fusion.80
  78.1 16.6 %all-to-all-start = ((bf16[2,1,256,128]{2,0,1,3:T(2,128)(2,1)}), bf16[2,1,256,128]{2,0,1,3:T(2,128)(2,1)S(1)}, u32[]{:S(2)}, u32[]{:S(2)}) async-start(bf16[2,1,256,128]{2,0,1,3:T(2,128)(2,1)} %copy.37), calls=%async_computation | async-start | bytes 262144 | tf_op jit(solution)/shard_map/all_to_all | solution.py:42
  96.1 15.3 %all-to-all-done = bf16[2,1,256,128]{2,0,1,3:T(2,128)(2,1)S(1)} async-done(((bf16[2,1,256,128]{2,0,1,3:T(2,128)(2,1)}), bf16[2,1,256,128]{2,0,1,3:T(2,128)(2,1)S(1)}, u32[]{:S(2)}, u32[]{:S(2)}) %all-to-all-start) | async-done | bytes 131104 | tf_op jit(solution)/shard_map/all_to_all | solution.py:42
  111.4 6.6 %all-to-all-start.2 = ((bf16[2,1,256,128]{2,0,1,3:T(2,128)(2,1)}), bf16[2,1,256,128]{2,0,1,3:T(2,128)(2,1)S(1)}, u32[]{:S(2)}, u32[]{:S(2)}) async-start(bf16[2,1,256,128]{2,0,1,3:T(2,128)(2,1)} %copy.43), calls=%async_computation.2 | async-start | bytes 262144 | tf_op jit(solution)/shard_map/all_to_all | solution.py:74
  118.1 10.0 %all_gather.6 = bf16[2,1,1024,128]{2,3,0,1:T(8,128)(2,1)S(1)} all-gather(bf16[2,1,256,128]{2,3,0,1:T(8,128)(2,1)S(1)} %copy.38), channel_id=1, replica_groups=mesh['y'=4,'x_lo'=2,'z'=16,'x_hi'=2,'core'=2] {'x_hi','core'}, dimensions={2}, use_global_device_ids=true | all-gather | bytes 655360 | tf_op jit(solution)/shard_map/all_gather | solution.py:46
  128.1 5.5 all-to-all-done.2
  133.6 11.5 %all_gather.7 = bf16[2,1,1024,128]{2,3,0,1:T(8,128)(2,1)S(1)} all-gather(bf16[2,1,256,128]{2,3,0,1:T(8,128)(2,1)S(1)} %copy.44), channel_id=1, replica_groups=mesh['y'=4,'x_lo'=2,'z'=16,'x_hi'=2,'core'=2] {'x_hi','core'}, dimensions={2}, use_global_device_ids=true | all-gather | bytes 655360 | tf_op jit(solution)/shard_map/all_gather | solution.py:78
  145.1 2.3 fusion.6
  147.4 1.0 copy-done.3
  148.4 1.6 fusion.14
  150.0 4.5 fusion.17
  154.5 52.4 %all-reduce.19.cloned.1.call-done = (bf16[1024,2,1,128]{0,3,1,2:T(8,128)(2,1)}, bf16[1024,2,1,128]{0,3,1,2:T(8,128)(2,1)}) async-done(((bf16[1024,2,1,128]{0,3,1,2:T(8,128)(2,1)}, bf16[1024,2,1,128]{0,3,1,2:T(8,128)(2,1)}), (bf16[1024,2,1,128]{0,3,1,2:T(8,128)(2,1)}, bf16[1024,2,1,128]{0,3,1,2:T(8,128)(2,1)})) %all-reduce.19.cloned.1.call-update) | async-done | bytes 1048592 | tf_op jit(solution)/shard_map/psum | solution.py:52
  207.0 0.9 convert_convert_fusion
  208.7 16.6 %all-to-all-start.3 = ((bf16[256,2,1,128]{0,1,2,3:T(2,128)(2,1)}), bf16[256,2,1,128]{0,1,2,3:T(2,128)(2,1)S(1)}, u32[]{:S(2)}, u32[]{:S(2)}) async-start(bf16[256,2,1,128]{0,1,2,3:T(2,128)(2,1)} %copy.45), calls=%async_computation.3 | async-start | bytes 262144 | tf_op jit(solution)/shard_map/all_to_all | solution.py:93
  225.3 0.9 convert_convert_fusion.1
  227.0 15.0 %all-to-all-done.3 = bf16[256,2,1,128]{0,1,2,3:T(2,128)(2,1)S(1)} async-done(((bf16[256,2,1,128]{0,1,2,3:T(2,128)(2,1)}), bf16[256,2,1,128]{0,1,2,3:T(2,128)(2,1)S(1)}, u32[]{:S(2)}, u32[]{:S(2)}) %all-to-all-start.3) | async-done | bytes 131104 | tf_op jit(solution)/shard_map/all_to_all | solution.py:93
  242.0 6.8 %all-to-all-start.1 = ((bf16[256,2,1,128]{0,1,2,3:T(2,128)(2,1)}), bf16[256,2,1,128]{0,1,2,3:T(2,128)(2,1)S(1)}, u32[]{:S(2)}, u32[]{:S(2)}) async-start(bf16[256,2,1,128]{0,1,2,3:T(2,128)(2,1)} %copy.39), calls=%async_computation.1 | async-start | bytes 262144 | tf_op jit(solution)/shard_map/all_to_all | solution.py:61
  250.3 14.1 %all-to-all-done.1 = bf16[256,2,1,128]{0,1,2,3:T(2,128)(2,1)S(1)} async-done(((bf16[256,2,1,128]{0,1,2,3:T(2,128)(2,1)}), bf16[256,2,1,128]{0,1,2,3:T(2,128)(2,1)S(1)}, u32[]{:S(2)}, u32[]{:S(2)}) %all-to-all-start.1) | async-done | bytes 131104 | tf_op jit(solution)/shard_map/all_to_all | solution.py:61
  265.8 48.2 %all-reduce.17.cloned.1.call-done = (bf16[1,196,256]{2,1,0:T(8,128)(2,1)}, bf16[1,196,256]{2,1,0:T(8,128)(2,1)}) async-done(((bf16[1,196,256]{2,1,0:T(8,128)(2,1)}, bf16[1,196,256]{2,1,0:T(8,128)(2,1)}), (bf16[1,196,256]{2,1,0:T(8,128)(2,1)}, bf16[1,196,256]{2,1,0:T(8,128)(2,1)})) %all-reduce.17.cloned.1.call-update) | async-done | bytes 200720 | tf_op jit(solution)/shard_map/psum | solution.py:99
  314.0 1.2 fusion.51
  315.2 1.1 fusion.65
  316.3 0.9 convolution_bitcast_fusion
  317.3 126.5 %all-reduce.11.cloned.1.call-done = f32[256,256]{0,1:T(8,128)} async-done(((f32[256,256]{0,1:T(8,128)}), f32[256,256]{0,1:T(8,128)}) %all-reduce.11.cloned.1.call-update) | async-done | bytes 262160 | tf_op jit(solution)/shard_map/psum | solution.py:112
  443.9 0.9 fusion.20
  444.8 62.7 %all-reduce.13.cloned.1.call-done = f32[256,256]{0,1:T(8,128)} async-done(((f32[256,256]{0,1:T(8,128)}), f32[256,256]{0,1:T(8,128)}) %all-reduce.13.cloned.1.call-update) | async-done | bytes 262160 | tf_op jit(solution)/shard_map/psum | solution.py:112
  507.7 0.9 fusion.21
  508.6 49.1 %all-reduce.15.cloned.1.call-done = f32[256,256]{0,1:T(8,128)} async-done(((f32[256,256]{0,1:T(8,128)}), f32[256,256]{0,1:T(8,128)}) %all-reduce.15.cloned.1.call-update) | async-done | bytes 262160 | tf_op jit(solution)/shard_map/psum | solution.py:112
  557.6 1.8 copy.52
  (66 shorter events, 7.6 us)
Async XLA Ops:
  7.2 141.2 %copy-start = (bf16[1,1024,1024]{2,1,0:T(8,128)(2,1)S(1)}, bf16[1,1024,1024]{2,1,0:T(8,128)(2,1)}, u32[]{:S(2)}) copy-start(bf16[1,1024,1024]{2,1,0:T(8,128)(2,1)} %param.8) | copy-start | bytes 6291460
  7.2 69.9 %copy-start.2 = (bf16[196,256]{1,0:T(8,128)(2,1)S(1)}, bf16[196,256]{1,0:T(8,128)(2,1)}, u32[]{:S(2)}) copy-start(bf16[196,256]{1,0:T(8,128)(2,1)} %param.5) | copy-start | bytes 301060
  7.2 87.9 %copy-start.5 = (bf16[196,256]{1,0:T(8,128)(2,1)S(1)}, bf16[196,256]{1,0:T(8,128)(2,1)}, u32[]{:S(2)}) copy-start(bf16[196,256]{1,0:T(8,128)(2,1)} %param.9) | copy-start | bytes 301060
  7.2 66.2 %all-reduce.9.cloned.1.call-start = ((), (), s32[]{:S(2)}) async-start(), calls=%async_computation.4 | async-start | bytes 409600 | tf_op jit(solution)/shard_map/psum | solution.py:34
  74.5 2.2 copy-start.7
  74.5 2.2 copy-start.9
  75.6 1.1 copy-start.11
  75.6 1.1 copy-start.13
  78.1 33.3 %all-to-all-start = ((bf16[2,1,256,128]{2,0,1,3:T(2,128)(2,1)}), bf16[2,1,256,128]{2,0,1,3:T(2,128)(2,1)S(1)}, u32[]{:S(2)}, u32[]{:S(2)}) async-start(bf16[2,1,256,128]{2,0,1,3:T(2,128)(2,1)} %copy.37), calls=%async_computation | async-start | bytes 262144 | tf_op jit(solution)/shard_map/all_to_all | solution.py:42
  111.4 22.2 %all-to-all-start.2 = ((bf16[2,1,256,128]{2,0,1,3:T(2,128)(2,1)}), bf16[2,1,256,128]{2,0,1,3:T(2,128)(2,1)S(1)}, u32[]{:S(2)}, u32[]{:S(2)}) async-start(bf16[2,1,256,128]{2,0,1,3:T(2,128)(2,1)} %copy.43), calls=%async_computation.2 | async-start | bytes 262144 | tf_op jit(solution)/shard_map/all_to_all | solution.py:74
  118.1 88.9 %all-reduce.19.cloned.1.call-start = ((), (), s32[]{:S(2)}) async-start(), calls=%async_computation.9 | async-start | bytes 2097152 | tf_op jit(solution)/shard_map/psum | solution.py:52
  147.4 1.0 copy-start.3
  154.5 110.0 %copy-start.6 = (bf16[196,256]{1,0:T(8,128)(2,1)S(1)}, bf16[196,256]{1,0:T(8,128)(2,1)}, u32[]{:S(2)}) copy-start(bf16[196,256]{1,0:T(8,128)(2,1)} %param.9) | copy-start | bytes 301060
  207.9 106.2 %copy-start.1 = (f32[1,196,256]{2,1,0:T(8,128)S(1)}, f32[1,196,256]{2,1,0:T(8,128)}, u32[]{:S(2)}) copy-start(f32[1,196,256]{2,1,0:T(8,128)} %all-reduce.9.cloned.1.call-done) | copy-start | bytes 602116
  207.9 106.1 %copy-start.8 = (f32[256]{0:T(256)S(1)}, f32[256]{0:T(256)}, u32[]{:S(2)}) copy-start(f32[256]{0:T(256)} %copy-done.7) | copy-start | bytes 3076
  207.9 106.1 %copy-start.10 = (f32[196]{0:T(256)S(1)}, f32[196]{0:T(256)}, u32[]{:S(2)}) copy-start(f32[196]{0:T(256)} %copy-done.9) | copy-start | bytes 2356
  207.9 106.1 %copy-start.12 = (f32[256]{0:T(256)S(1)}, f32[256]{0:T(256)}, u32[]{:S(2)}) copy-start(f32[256]{0:T(256)} %copy-done.11) | copy-start | bytes 3076
  207.9 106.1 %copy-start.14 = (f32[196]{0:T(256)S(1)}, f32[196]{0:T(256)}, u32[]{:S(2)}) copy-start(f32[196]{0:T(256)} %copy-done.13) | copy-start | bytes 2356
  208.7 33.3 %all-to-all-start.3 = ((bf16[256,2,1,128]{0,1,2,3:T(2,128)(2,1)}), bf16[256,2,1,128]{0,1,2,3:T(2,128)(2,1)S(1)}, u32[]{:S(2)}, u32[]{:S(2)}) async-start(bf16[256,2,1,128]{0,1,2,3:T(2,128)(2,1)} %copy.45), calls=%async_computation.3 | async-start | bytes 262144 | tf_op jit(solution)/shard_map/all_to_all | solution.py:93
  242.0 22.3 %all-to-all-start.1 = ((bf16[256,2,1,128]{0,1,2,3:T(2,128)(2,1)}), bf16[256,2,1,128]{0,1,2,3:T(2,128)(2,1)S(1)}, u32[]{:S(2)}, u32[]{:S(2)}) async-start(bf16[256,2,1,128]{0,1,2,3:T(2,128)(2,1)} %copy.39), calls=%async_computation.1 | async-start | bytes 262144 | tf_op jit(solution)/shard_map/all_to_all | solution.py:61
  248.8 65.2 %all-reduce.17.cloned.1.call-start = ((), (), s32[]{:S(2)}) async-start(), calls=%async_computation.8 | async-start | bytes 409600 | tf_op jit(solution)/shard_map/psum | solution.py:99
  264.5 243.2 %copy-start.4 = (bf16[256,256]{1,0:T(8,128)(2,1)S(1)}, bf16[256,256]{1,0:T(8,128)(2,1)}, u32[]{:S(2)}) copy-start(bf16[256,256]{1,0:T(8,128)(2,1)} %param.6) | copy-start | bytes 393220
  265.8 178.0 %all-reduce.11.cloned.1.call-start = ((), (), s32[]{:S(2)}) async-start(), calls=%async_computation.5 | async-start | bytes 524288 | tf_op jit(solution)/shard_map/psum | solution.py:112
  317.3 190.1 %all-reduce.13.cloned.1.call-start = ((), (), s32[]{:S(2)}) async-start(), calls=%async_computation.6 | async-start | bytes 524288 | tf_op jit(solution)/shard_map/psum | solution.py:112
  443.9 113.8 %all-reduce.15.cloned.1.call-start = ((), (), s32[]{:S(2)}) async-start(), calls=%async_computation.7 | async-start | bytes 524288 | tf_op jit(solution)/shard_map/psum | solution.py:112
Sparse Core Ops, SparseCore 0:
  11.5 61.8 all-reduce.8
  154.7 52.2 all-reduce.18
  265.9 48.0 all-reduce.16
  317.4 126.3 all-reduce.10
  446.0 61.3 all-reduce.12
  510.2 47.4 all-reduce.14
where the time goes:
time: 567 us; the launch traced here: 566 us
  waiting for transfers between devices  453 us (80%)
  starting transfers between devices  46.9 us (8%)
  blocking collectives  21.4 us (4%)
  between operations  14.5 us (3%)
  matrix products  14.1 us (2%)
  local copies, waits for them, and re-layouts  8.99 us (2%)
  other arithmetic  7.34 us (1%)
    psum x3, waiting for transfers between devices, local(): grad_params = lax.psum(lax.psum(lax.psum(params_part, 'z'), 'y'), 'x_lo')  238 us
    psum x1, waiting for transfers between devices, local(): logits = lax.psum(partial_logits, HALF)  64.2 us
    psum x1, waiting for transfers between devices, local(): lax.psum(jnp.einsum('kf,sirk->fsir', down_slice, hidden, preferred_elemen...  52.4 us
    psum x1, waiting for transfers between devices, local(): lax.psum(dispatch_part.astype(jnp.bfloat16), HALF).astype(jnp.float32)  48.2 us
    all_to_all x1, starting transfers between devices, local(): lax.all_to_all(grad_slot_in.astype(jnp.bfloat16), EXPERT, split_axis=3, c...  16.6 us
    all_to_all x1, starting transfers between devices, local(): lax.all_to_all(slot_in, EXPERT, split_axis=3, concat_axis=3, tiled=True)  16.6 us
    all_to_all x1, waiting for transfers between devices, local(): lax.all_to_all(slot_in, EXPERT, split_axis=3, concat_axis=3, tiled=True)  15.3 us
    all_to_all x1, waiting for transfers between devices, local(): lax.all_to_all(grad_slot_in.astype(jnp.bfloat16), EXPERT, split_axis=3, c...  15 us
  transfers between devices with their start and end apart: 10, of which 10 were waited for; matrix products, arithmetic and copies ran while one was open for 1% of the time, Pallas kernels for 0%

commit v1 on v0

--- a/solution.py
+++ b/solution.py
@@ -31,7 +31,7 @@
     partial_logits = jnp.einsum(
         "imf,fc->imc", inputs, slot_params, preferred_element_type=jnp.float32
     )
-    logits = lax.psum(partial_logits, HALF)
+    logits = jnp.sum(lax.all_gather(partial_logits, HALF), axis=0)
     dispatch = jax.nn.softmax(logits, axis=1)
     combine = jax.nn.softmax(logits, axis=2)
     dispatch_bf = dispatch.astype(jnp.bfloat16).reshape(images, SEQ, experts, SLOTS)

time: 567 us -> 515 us (0.908)
  waiting for transfers between devices: 453 us -> 388 us
  blocking collectives: 21.4 us -> 38.5 us
    psum x1 -> x0, waiting for transfers between devices: 64.2 us -> none  [local(): logits = lax.psum(partial_logits, HALF)]
    all_gather x0 -> x1, blocking collectives: none -> 15.6 us  [local(): logits = jnp.sum(lax.all_gather(partial_logits, HALF), axis=0)]
  transfers between devices with their start and end apart: 10 -> 9, of which waited for: 10 -> 9; matrix products, arithmetic and copies ran while one was open for 1% -> 1% of each run, Pallas kernels for 0% -> 0%
where the time goes in v1:
time: 515 us
  waiting for transfers between devices  388 us (75%)
  starting transfers between devices  46.4 us (9%)
  blocking collectives  38.5 us (7%)
  between operations  14.1 us (3%)
  matrix products  13.5 us (3%)
  local copies, waits for them, and re-layouts  9.18 us (2%)
  other arithmetic  5.36 us (1%)
    psum x3, waiting for transfers between devices, local(): grad_params = lax.psum(lax.psum(lax.psum(params_part, 'z'), 'y'), 'x_lo')  238 us
    psum x1, waiting for transfers between devices, local(): lax.psum(jnp.einsum('kf,sirk->fsir', down_slice, hidden, preferred_elemen...  52.6 us
    psum x1, waiting for transfers between devices, local(): lax.psum(dispatch_part.astype(jnp.bfloat16), HALF).astype(jnp.float32)  48.2 us
    all_to_all x1, starting transfers between devices, local(): lax.all_to_all(grad_slot_in.astype(jnp.bfloat16), EXPERT, split_axis=3, c...  16.6 us
    all_to_all x1, starting transfers between devices, local(): lax.all_to_all(slot_in, EXPERT, split_axis=3, concat_axis=3, tiled=True)  16.3 us
    all_gather x1, blocking collectives, local(): logits = jnp.sum(lax.all_gather(partial_logits, HALF), axis=0)  15.6 us
    all_to_all x1, waiting for transfers between devices, local(): lax.all_to_all(slot_in, EXPERT, split_axis=3, concat_axis=3, tiled=True)  15 us
    all_to_all x1, waiting for transfers between devices, local(): lax.all_to_all(grad_slot_in.astype(jnp.bfloat16), EXPERT, split_axis=3, c...  15 us
  transfers between devices with their start and end apart: 9, of which 9 were waited for; matrix products, arithmetic and copies ran while one was open for 1% of the time, Pallas kernels for 0%

profile of v1, /device:TPU:1, one launch (start us, length us, event | category | flops | bytes accessed | tf_op | source)
XLA Modules:
  0.0 514.9 jit_solution(17306503490912330313)
XLA Ops:
  7.2 1.3 convolution_bitcast_fusion.3
  8.5 15.6 %all-gather.1 = f32[4,196,256]{2,1,0:T(8,128)S(1)} all-gather(f32[1,196,256]{2,1,0:T(8,128)S(1)} %convolution_bitcast_fusion.3), channel_id=2, replica_groups=mesh['y'=4,'x_lo'=2,'z'=16,'x_hi'=2,'core'=2] {'x_hi','core'}, dimensions={0}, use_global_device_ids=true | all-gather | bytes 1003520 | tf_op jit(solution)/shard_map/all_gather | solution.py:34
  25.9 0.8 copy.45
  26.7 16.3 %all-to-all-start = ((bf16[2,1,256,128]{2,0,1,3:T(2,128)(2,1)}), bf16[2,1,256,128]{2,0,1,3:T(2,128)(2,1)S(1)}, u32[]{:S(2)}, u32[]{:S(2)}) async-start(bf16[2,1,256,128]{2,0,1,3:T(2,128)(2,1)} %copy.45), calls=%async_computation | async-start | bytes 262144 | tf_op jit(solution)/shard_map/all_to_all | solution.py:42
  44.7 15.0 %all-to-all-done = bf16[2,1,256,128]{2,0,1,3:T(2,128)(2,1)S(1)} async-done(((bf16[2,1,256,128]{2,0,1,3:T(2,128)(2,1)}), bf16[2,1,256,128]{2,0,1,3:T(2,128)(2,1)S(1)}, u32[]{:S(2)}, u32[]{:S(2)}) %all-to-all-start) | async-done | bytes 131104 | tf_op jit(solution)/shard_map/all_to_all | solution.py:42
  59.7 6.6 %all-to-all-start.2 = ((bf16[2,1,256,128]{2,0,1,3:T(2,128)(2,1)}), bf16[2,1,256,128]{2,0,1,3:T(2,128)(2,1)S(1)}, u32[]{:S(2)}, u32[]{:S(2)}) async-start(bf16[2,1,256,128]{2,0,1,3:T(2,128)(2,1)} %copy.51), calls=%async_computation.2 | async-start | bytes 262144 | tf_op jit(solution)/shard_map/all_to_all | solution.py:74
  66.4 10.7 %all_gather.14 = bf16[2,1,1024,128]{2,3,0,1:T(8,128)(2,1)S(1)} all-gather(bf16[2,1,256,128]{2,3,0,1:T(8,128)(2,1)S(1)} %copy.46), channel_id=1, replica_groups=mesh['y'=4,'x_lo'=2,'z'=16,'x_hi'=2,'core'=2] {'x_hi','core'}, dimensions={2}, use_global_device_ids=true | all-gather | bytes 655360 | tf_op jit(solution)/shard_map/all_gather | solution.py:46
  77.0 4.8 all-to-all-done.2
  81.9 12.3 %all_gather.15 = bf16[2,1,1024,128]{2,3,0,1:T(8,128)(2,1)} all-gather(bf16[2,1,256,128]{2,3,0,1:T(8,128)(2,1)S(1)} %copy.52), channel_id=1, replica_groups=mesh['y'=4,'x_lo'=2,'z'=16,'x_hi'=2,'core'=2] {'x_hi','core'}, dimensions={2}, use_global_device_ids=true | all-gather | bytes 655360 | tf_op jit(solution)/shard_map/all_gather | solution.py:78
  94.1 2.3 fusion.6
  96.4 1.0 copy-done.2
  97.4 1.6 fusion.14
  99.1 4.5 fusion.17
  103.6 52.6 %all-reduce.16.cloned.1.call-done = (bf16[1024,2,1,128]{0,3,1,2:T(8,128)(2,1)}, bf16[1024,2,1,128]{0,3,1,2:T(8,128)(2,1)}) async-done(((bf16[1024,2,1,128]{0,3,1,2:T(8,128)(2,1)}, bf16[1024,2,1,128]{0,3,1,2:T(8,128)(2,1)}), (bf16[1024,2,1,128]{0,3,1,2:T(8,128)(2,1)}, bf16[1024,2,1,128]{0,3,1,2:T(8,128)(2,1)})) %all-reduce.16.cloned.1.call-update) | async-done | bytes 1048592 | tf_op jit(solution)/shard_map/psum | solution.py:52
  156.2 0.9 convert_convert_fusion
  157.1 0.8 copy.53
  157.9 16.6 %all-to-all-start.3 = ((bf16[256,2,1,128]{0,1,2,3:T(2,128)(2,1)}), bf16[256,2,1,128]{0,1,2,3:T(2,128)(2,1)S(1)}, u32[]{:S(2)}, u32[]{:S(2)}) async-start(bf16[256,2,1,128]{0,1,2,3:T(2,128)(2,1)} %copy.53), calls=%async_computation.3 | async-start | bytes 262144 | tf_op jit(solution)/shard_map/all_to_all | solution.py:93
  174.5 0.9 convert_convert_fusion.1
  175.4 0.8 copy.47
  176.2 15.0 %all-to-all-done.3 = bf16[256,2,1,128]{0,1,2,3:T(2,128)(2,1)S(1)} async-done(((bf16[256,2,1,128]{0,1,2,3:T(2,128)(2,1)}), bf16[256,2,1,128]{0,1,2,3:T(2,128)(2,1)S(1)}, u32[]{:S(2)}, u32[]{:S(2)}) %all-to-all-start.3) | async-done | bytes 131104 | tf_op jit(solution)/shard_map/all_to_all | solution.py:93
  191.2 6.6 %all-to-all-start.1 = ((bf16[256,2,1,128]{0,1,2,3:T(2,128)(2,1)}), bf16[256,2,1,128]{0,1,2,3:T(2,128)(2,1)S(1)}, u32[]{:S(2)}, u32[]{:S(2)}) async-start(bf16[256,2,1,128]{0,1,2,3:T(2,128)(2,1)} %copy.47), calls=%async_computation.1 | async-start | bytes 262144 | tf_op jit(solution)/shard_map/all_to_all | solution.py:61
  199.3 14.1 %all-to-all-done.1 = bf16[256,2,1,128]{0,1,2,3:T(2,128)(2,1)S(1)} async-done(((bf16[256,2,1,128]{0,1,2,3:T(2,128)(2,1)}), bf16[256,2,1,128]{0,1,2,3:T(2,128)(2,1)S(1)}, u32[]{:S(2)}, u32[]{:S(2)}) %all-to-all-start.1) | async-done | bytes 131104 | tf_op jit(solution)/shard_map/all_to_all | solution.py:61
  214.8 48.2 %all-reduce.14.cloned.1.call-done = (bf16[1,196,256]{2,1,0:T(8,128)(2,1)}, bf16[1,196,256]{2,1,0:T(8,128)(2,1)}) async-done(((bf16[1,196,256]{2,1,0:T(8,128)(2,1)}, bf16[1,196,256]{2,1,0:T(8,128)(2,1)}), (bf16[1,196,256]{2,1,0:T(8,128)(2,1)}, bf16[1,196,256]{2,1,0:T(8,128)(2,1)})) %all-reduce.14.cloned.1.call-update) | async-done | bytes 200720 | tf_op jit(solution)/shard_map/psum | solution.py:99
  263.0 1.2 fusion.52
  264.2 1.1 fusion.67
  265.3 0.9 convolution_bitcast_fusion
  266.3 126.5 %all-reduce.8.cloned.1.call-done = f32[256,256]{0,1:T(8,128)} async-done(((f32[256,256]{0,1:T(8,128)}), f32[256,256]{0,1:T(8,128)}) %all-reduce.8.cloned.1.call-update) | async-done | bytes 262160 | tf_op jit(solution)/shard_map/psum | solution.py:112
  392.9 0.9 fusion.20
  393.8 62.7 %all-reduce.10.cloned.1.call-done = f32[256,256]{0,1:T(8,128)} async-done(((f32[256,256]{0,1:T(8,128)}), f32[256,256]{0,1:T(8,128)}) %all-reduce.10.cloned.1.call-update) | async-done | bytes 262160 | tf_op jit(solution)/shard_map/psum | solution.py:112
  456.7 0.9 fusion.21
  457.6 49.1 %all-reduce.12.cloned.1.call-done = f32[256,256]{0,1:T(8,128)} async-done(((f32[256,256]{0,1:T(8,128)}), f32[256,256]{0,1:T(8,128)}) %all-reduce.12.cloned.1.call-update) | async-done | bytes 262160 | tf_op jit(solution)/shard_map/psum | solution.py:112
  506.6 1.8 copy.60
  (49 shorter events, 6.6 us)
Async XLA Ops:
  7.2 90.3 %copy-start = (bf16[1,1024,1024]{2,1,0:T(8,128)(2,1)S(1)}, bf16[1,1024,1024]{2,1,0:T(8,128)(2,1)}, u32[]{:S(2)}) copy-start(bf16[1,1024,1024]{2,1,0:T(8,128)(2,1)} %param.8) | copy-start | bytes 6291460
  8.5 17.2 %copy-start.1 = (bf16[196,256]{1,0:T(8,128)(2,1)S(1)}, bf16[196,256]{1,0:T(8,128)(2,1)}, u32[]{:S(2)}) copy-start(bf16[196,256]{1,0:T(8,128)(2,1)} %param.5) | copy-start | bytes 301060
  24.2 19.5 %copy-start.5 = (bf16[196,256]{1,0:T(8,128)(2,1)S(1)}, bf16[196,256]{1,0:T(8,128)(2,1)}, u32[]{:S(2)}) copy-start(bf16[196,256]{1,0:T(8,128)(2,1)} %param.9) | copy-start | bytes 301060
  26.7 33.0 %all-to-all-start = ((bf16[2,1,256,128]{2,0,1,3:T(2,128)(2,1)}), bf16[2,1,256,128]{2,0,1,3:T(2,128)(2,1)S(1)}, u32[]{:S(2)}, u32[]{:S(2)}) async-start(bf16[2,1,256,128]{2,0,1,3:T(2,128)(2,1)} %copy.45), calls=%async_computation | async-start | bytes 262144 | tf_op jit(solution)/shard_map/all_to_all | solution.py:42
  59.7 22.2 %all-to-all-start.2 = ((bf16[2,1,256,128]{2,0,1,3:T(2,128)(2,1)}), bf16[2,1,256,128]{2,0,1,3:T(2,128)(2,1)S(1)}, u32[]{:S(2)}, u32[]{:S(2)}) async-start(bf16[2,1,256,128]{2,0,1,3:T(2,128)(2,1)} %copy.51), calls=%async_computation.2 | async-start | bytes 262144 | tf_op jit(solution)/shard_map/all_to_all | solution.py:74
  66.3 89.9 %all-reduce.16.cloned.1.call-start = ((), (), s32[]{:S(2)}) async-start(), calls=%async_computation.8 | async-start | bytes 2097152 | tf_op jit(solution)/shard_map/psum | solution.py:52
  96.4 1.0 copy-start.2
  97.4 1.6 copy-start.3
  157.9 33.3 %all-to-all-start.3 = ((bf16[256,2,1,128]{0,1,2,3:T(2,128)(2,1)}), bf16[256,2,1,128]{0,1,2,3:T(2,128)(2,1)S(1)}, u32[]{:S(2)}, u32[]{:S(2)}) async-start(bf16[256,2,1,128]{0,1,2,3:T(2,128)(2,1)} %copy.53), calls=%async_computation.3 | async-start | bytes 262144 | tf_op jit(solution)/shard_map/all_to_all | solution.py:93
  191.2 22.1 %all-to-all-start.1 = ((bf16[256,2,1,128]{0,1,2,3:T(2,128)(2,1)}), bf16[256,2,1,128]{0,1,2,3:T(2,128)(2,1)S(1)}, u32[]{:S(2)}, u32[]{:S(2)}) async-start(bf16[256,2,1,128]{0,1,2,3:T(2,128)(2,1)} %copy.47), calls=%async_computation.1 | async-start | bytes 262144 | tf_op jit(solution)/shard_map/all_to_all | solution.py:61
  197.8 65.2 %all-reduce.14.cloned.1.call-start = ((), (), s32[]{:S(2)}) async-start(), calls=%async_computation.7 | async-start | bytes 409600 | tf_op jit(solution)/shard_map/psum | solution.py:99
  213.5 243.2 %copy-start.4 = (bf16[256,256]{1,0:T(8,128)(2,1)S(1)}, bf16[256,256]{1,0:T(8,128)(2,1)}, u32[]{:S(2)}) copy-start(bf16[256,256]{1,0:T(8,128)(2,1)} %param.6) | copy-start | bytes 393220
  214.8 178.0 %all-reduce.8.cloned.1.call-start = ((), (), s32[]{:S(2)}) async-start(), calls=%async_computation.4 | async-start | bytes 524288 | tf_op jit(solution)/shard_map/psum | solution.py:112
  266.3 190.2 %all-reduce.10.cloned.1.call-start = ((), (), s32[]{:S(2)}) async-start(), calls=%async_computation.5 | async-start | bytes 524288 | tf_op jit(solution)/shard_map/psum | solution.py:112
  392.8 113.8 %all-reduce.12.cloned.1.call-start = ((), (), s32[]{:S(2)}) async-start(), calls=%async_computation.6 | async-start | bytes 524288 | tf_op jit(solution)/shard_map/psum | solution.py:112
Sparse Core Ops, SparseCore 0:
  103.7 52.4 all-reduce.15
  214.9 48.0 all-reduce.13
  266.4 126.3 all-reduce.7
  395.0 61.3 all-reduce.9
  459.1 47.4 all-reduce.11
